TPU v7x, 32 devices: a whole 2x2x4 slice. The times are simulated.
32 devices in a mesh: space: 4 (over y, core), tm: 8 (over z, x).
Axes of the slice: x: 2, y: 2, z: 4, core: 2. Of those that a mesh axis runs over, the one named last changes fastest.
Arguments:
- snapshots: float32 [2048, 30720], P('tm', 'space'), may hold values from -6 to 6
- closing: float32 [128, 30720], P(None, 'space'), may hold values from -6 to 6
- weights: float32 [30720], P('space'), may hold values from 0.25 to 36, as said below
- bin_index: int32 [64], replicated, may hold values from 0 to 128, as said below
Outputs:
- spectra: float32 [64, 2, 16, 16], P('tm', None, 'space')
Inputs may be any that keep to these rules, and one draw needn't show every extreme that they name: `bin_index`: distinct bins. Positive weights.
All inputs are finite; a program needn't handle non-finite values.
Results may differ from a plain program's by a relative error of at most 0.0003.
Values sent between devices are 32-bit elements; how exact they have to be, the bound alone decides.
A program may use at most 128 MiB of HBM per device.

v0:
```python
import jax
import jax.numpy as jnp
from jax import lax
from jax.sharding import PartitionSpec as P

NFFT = 256
NBINS = 64


def passed_along(array, axis, by):
    peers = lax.axis_size(axis)
    pairs = [(i, i + by) for i in range(peers) if 0 <= i + by < peers]
    return lax.ppermute(array, axis, pairs)


def spectral_table(bin_index, length):
    sample = jnp.arange(length, dtype=jnp.int32)
    window = 0.5 - 0.5 * jnp.cos(2.0 * jnp.pi * sample.astype(jnp.float32) / length)
    phase_turns = sample[:, None] * bin_index[None, :] % length
    phase_angle = 2.0 * jnp.pi * phase_turns.astype(jnp.float32) / length
    paired = jnp.stack(
        [window[:, None] * jnp.cos(phase_angle), -window[:, None] * jnp.sin(phase_angle)], axis=2
    )
    return paired.reshape(length, 2 * bin_index.shape[0])


def cross_spectra(first_set, second_set):
    products = jnp.einsum(
        "kaip,kbjp->kabij", first_set, second_set, precision=lax.Precision.HIGHEST
    )
    real_part = products[:, 0, 0] + products[:, 1, 1]
    imag_part = products[:, 0, 1] - products[:, 1, 0]
    return jnp.stack([real_part, imag_part], axis=1)


def body(snapshots, closing, weights, bin_index):
    stride_rows = NFFT // 2
    tail_rows = closing.shape[0]
    blocks_here = snapshots.shape[0] // stride_rows
    points = snapshots.shape[1]
    width_tm = lax.axis_size("tm")
    width_space = lax.axis_size("space")
    blocks_all = blocks_here * width_tm
    own_rows = blocks_all // width_space
    basis_table = spectral_table(bin_index, NFFT)
    incoming = passed_along(snapshots[:tail_rows], "tm", -1)
    last_device = lax.axis_index("tm") == width_tm - 1
    series = jnp.concatenate([snapshots, jnp.where(last_device, closing, incoming)], axis=0)
    leading = series[: blocks_here * stride_rows].reshape(blocks_here, stride_rows, points)
    trailing = series[stride_rows:].reshape(blocks_here, stride_rows, points)
    pieces = jnp.concatenate([leading, trailing], axis=1)
    spectrum = jnp.einsum("nc,bnp->cbp", basis_table, pieces, precision=lax.Precision.HIGHEST)
    spectrum = spectrum.reshape(NBINS, 2, blocks_here, points)
    gathered = lax.all_to_all(spectrum, "tm", split_axis=0, concat_axis=2, tiled=True)
    weighted = gathered * weights
    summed = lax.psum_scatter(
        cross_spectra(gathered, weighted).transpose(2, 0, 1, 3),
        "space",
        scatter_dimension=0,
        tiled=True,
    )
    row_ids = lax.axis_index("space") * own_rows + jnp.arange(own_rows, dtype=jnp.int32)
    diagonal = (row_ids[:, None] == jnp.arange(blocks_all, dtype=jnp.int32)[None, :]).astype(
        jnp.float32
    )
    local_trace = jnp.einsum(
        "rkj,rj->k", summed[:, :, 0, :], diagonal, precision=lax.Precision.HIGHEST
    )
    energy = lax.psum(local_trace, "space")
    spectra = summed * (blocks_all / energy)[None, :, None, None]
    return spectra.transpose(1, 2, 0, 3)


def solution(mesh):
    return jax.shard_map(
        body,
        mesh=mesh,
        in_specs=(P("tm", "space"), P(None, "space"), P("space"), P()),
        out_specs=P("tm", None, "space", None),
        check_vma=False,
    )
```

profile of v0, /device:TPU:0, one launch (start us, length us, event | category | flops | bytes accessed | tf_op | source)
XLA Modules:
  0.0 407.1 jit_solution(13800069312706185596)
XLA Ops:
  6.5 0.0 copy-start.1
  6.5 4.3 %slice.21 = f32[128,7680]{1,0:T(8,128)} slice(f32[256,7680]{1,0:T(8,128)} %param.4), slice={[0:128], [0:7680]} | slice | bytes 7864320 | tf_op jit(solution)/shard_map/slice | solution.py:46
  10.8 1.3 collective-permute-start
  12.2 0.0 copy-done.1
  12.2 0.3 cosine_multiply_fusion
  12.5 0.1 copy.21
  12.6 0.1 reshape.206
  12.7 0.1 dot_general.14
  12.8 88.1 %collective-permute-done = f32[128,7680]{1,0:T(8,128)} collective-permute-done((f32[128,7680]{1,0:T(8,128)}, f32[128,7680]{1,0:T(8,128)}, u32[]{:S(2)}, u32[]{:S(2)}) %collective-permute-start) | collective-permute-done | bytes 3932192 | tf_op jit(solution)/shard_map/ppermute | solution.py:13
  100.9 0.0 slice-start
  100.9 4.5 %broadcast_select_fusion = f32[128,7680]{1,0:T(8,128)} fusion(f32[128,7680]{1,0:T(8,128)} %param.5, f32[128,7680]{1,0:T(8,128)} %collective-permute-done, pred[]{:T(512)S(6)} %eq.18), kind=kLoop, calls=%fused_computation.11 | loop fusion | flops 983040 | bytes 11796481 | tf_op jit(solution)/shard_map/jit(_where)/select_n | solution.py:48
  105.5 4.0 pad_maximum_fusion
  109.5 0.0 slice-done
  109.5 0.3 slice-done.1
  109.8 10.9 %fusion = f32[64,2,2,7680]{3,0,2,1:T(8,128)} fusion(f32[2,128,7680]{2,1,0:T(8,128)S(1)} %bitcast.57, f32[2,128,7680]{2,1,0:T(8,128)S(1)} %bitcast.56, f32[64,2,256,1]{2,1,0,3:T(2,128)S(1)} %bitcast.58), kind=kOutput, calls=%fused_computation.1 | convolution fusion | flops 6043729920 | bytes 23724032 | tf_op jit(solution)/shard_map/nc,bnp->cbp/dot_general | solution.py:52
  120.7 12.3 %copy.23 = f32[64,2,2,7680]{3,2,1,0:T(2,128)} copy(f32[64,2,2,7680]{3,0,2,1:T(8,128)} %fusion) | data formatting | bytes 15728640 | tf_op jit(solution)/shard_map/nc,bnp->cbp/dot_general | solution.py:52
  133.0 5.9 %all-to-all-start = ((f32[64,2,2,7680]{3,2,1,0:T(2,128)}), f32[64,2,2,7680]{3,2,1,0:T(2,128)}, u32[]{:S(2)}, u32[]{:S(2)}) async-start(f32[64,2,2,7680]{3,2,1,0:T(2,128)} %copy.23), calls=%async_computation | async-start | bytes 15728640 | tf_op jit(solution)/shard_map/all_to_all | solution.py:54
  139.0 0.0 reduce-scatter.2.cloned.1.call-start
  139.0 171.0 %all-to-all-done = f32[64,2,2,7680]{3,2,1,0:T(2,128)} async-done(((f32[64,2,2,7680]{3,2,1,0:T(2,128)}), f32[64,2,2,7680]{3,2,1,0:T(2,128)}, u32[]{:S(2)}, u32[]{:S(2)}) %all-to-all-start) | async-done | bytes 7864352 | tf_op jit(solution)/shard_map/all_to_all | solution.py:54
  310.1 7.1 %copy.42 = f32[8,8,2,2,7680]{4,3,0,2,1:T(2,128)} copy(f32[8,8,2,2,7680]{4,3,2,1,0:T(2,128)} %bitcast.5) | data formatting | bytes 15728640 | tf_op jit(solution)/shard_map/all_to_all | solution.py:54
  317.2 9.9 %reshape.212 = f32[8,2,16,7680,1]{3,2,1,0,4:T(8,128)} reshape(f32[8,2,8,2,7680]{4,3,2,1,0:T(2,128)} %bitcast.52) | data formatting | bytes 15728640 | tf_op jit(solution)/shard_map/all_to_all | solution.py:54
  327.1 10.0 %all_to_all.16 = f32[8,2,16,7680]{3,2,1,0:T(8,128)} reshape(f32[8,2,8,2,7680]{4,3,2,1,0:T(2,128)} %bitcast.53) | data formatting | bytes 15728640 | tf_op jit(solution)/shard_map/all_to_all | solution.py:54
  337.1 0.0 copy-done
  337.1 35.3 %fusion.8 = f32[8,2,2,16,16]{3,4,1,2,0:T(8,128)S(1)} fusion(f32[8,2,16,7680,1]{3,2,1,0,4:T(8,128)} %reshape.212, f32[8,2,16,7680]{3,2,1,0:T(8,128)} %all_to_all.16, f32[7680]{0:T(1024)S(1)} %copy-done), kind=kOutput, calls=%fused_computation.12 | convolution fusion | flops 756940800 | bytes 15792128 | tf_op jit(solution)/shard_map/kaip,kbjp->kabij/dot_general | solution.py:28
  372.5 0.8 copy.27
  373.2 0.0 reduce-scatter.2.cloned.1.call-update
  373.3 0.1 fusion.24
  373.3 18.8 %reduce-scatter.2.cloned.1.call-done = f32[4,8,2,16]{3,1,2,0:T(8,128)} async-done(((f32[16,8,2,16]{3,1,2,0:T(8,128)}), f32[4,8,2,16]{3,1,2,0:T(8,128)}) %reduce-scatter.2.cloned.1.call-update) | async-done | bytes 4112 | tf_op jit(solution)/shard_map/reduce_scatter | solution.py:56
  392.2 0.8 convolution_bitcast_fusion
  393.0 5.7 %psum.7 = f32[8]{0:T(128)S(1)} all-reduce(f32[8]{0:T(128)S(1)} %convolution_bitcast_fusion), channel_id=1, replica_groups=mesh['space'=4,'tm'=8] {'space'}, use_global_device_ids=true, to_apply=%region_1.2 | all-reduce | flops 8 | bytes 64 | tf_op jit(solution)/shard_map/psum | solution.py:69
  398.7 0.8 multiply_bitcast_fusion
  399.6 0.6 copy.28
  (10 shorter events, 0.1 us)
Async XLA Ops:
  6.5 5.6 %copy-start.1 = (s32[64]{0:T(128)S(1)}, s32[64]{0:T(128)}, u32[]{:S(2)}) copy-start(s32[64]{0:T(128)} %param.7) | copy-start | bytes 772
  10.8 90.1 %collective-permute-start = (f32[128,7680]{1,0:T(8,128)}, f32[128,7680]{1,0:T(8,128)}, u32[]{:S(2)}, u32[]{:S(2)}) collective-permute-start(f32[128,7680]{1,0:T(8,128)} %slice.21), channel_id=1, source_target_pairs={{1,0},{2,1},{3,2},{4,3},{5,4},{6,5},{7,6},{9,8},{10,9},{11,10},{12... | collective-permute-start | bytes 11796488 | tf_op jit(solution)/shard_map/ppermute | solution.py:13
  100.9 8.5 %slice-start = ((s8[7864320]{0:T(1024)(128)(4,1)}), s8[4194304]{0:T(1024)(128)(4,1)S(1)}, s32[]{:S(2)}) async-start(s8[7864320]{0:T(1024)(128)(4,1)} %bitcast.54), calls=%async_computation.3 | async-start | bytes 8388608
  105.5 4.3 %slice-start.1 = ((s8[7864320]{0:T(1024)(128)(4,1)}), s8[3670016]{0:T(1024)(128)(4,1)S(1)}, s32[]{:S(2)}) async-start(s8[7864320]{0:T(1024)(128)(4,1)} %bitcast.54), calls=%async_computation.4 | async-start | bytes 7340032
  133.0 177.0 %all-to-all-start = ((f32[64,2,2,7680]{3,2,1,0:T(2,128)}), f32[64,2,2,7680]{3,2,1,0:T(2,128)}, u32[]{:S(2)}, u32[]{:S(2)}) async-start(f32[64,2,2,7680]{3,2,1,0:T(2,128)} %copy.23), calls=%async_computation | async-start | bytes 15728640 | tf_op jit(solution)/shard_map/all_to_all | solution.py:54
  139.0 253.2 %reduce-scatter.2.cloned.1.call-start = ((), (), s32[]{:S(2)}) async-start(), calls=%async_computation.2 | async-start | bytes 163840 | tf_op jit(solution)/shard_map/reduce_scatter | solution.py:56
  327.1 10.0 %copy-start = (f32[7680]{0:T(1024)S(1)}, f32[7680]{0:T(1024)}, u32[]{:S(2)}) copy-start(f32[7680]{0:T(1024)} %param.6) | copy-start | bytes 92164
Sparse Core Ops, SparseCore 0:
  373.4 18.7 reduce-scatter.1
where the time goes:
time: 408 us; the launch traced here: 407 us
  waiting for transfers between devices  278 us (68%)
  matrix products  47 us (12%)
  local copies, waits for them, and re-layouts  45.6 us (11%)
  between operations  13.5 us (3%)
  other arithmetic  9.88 us (2%)
  starting transfers between devices  7.25 us (2%)
  blocking collectives  5.74 us (1%)
    all_to_all x1, waiting for transfers between devices, body(): lax.all_to_all(spectrum, 'tm', split_axis=0, concat_axis=2, tiled=True)  171 us
    ppermute x1, waiting for transfers between devices, passed_along(): return lax.ppermute(array, axis, pairs)  88.1 us
    dot_general x1, matrix products, cross_spectra(): jnp.einsum('kaip,kbjp->kabij', first_set, second_set, precision=lax.Preci...  35.3 us
    all_to_all x3, local copies, waits for them, and re-layouts, body(): lax.all_to_all(spectrum, 'tm', split_axis=0, concat_axis=2, tiled=True)  27 us
    reduce_scatter x1, waiting for transfers between devices, body(): lax.psum_scatter(cross_spectra(gathered, weighted).transpose(2, 0, 1, 3),...  18.8 us
    dot_general x2, local copies, waits for them, and re-layouts, body(): jnp.einsum('nc,bnp->cbp', basis_table, pieces, precision=lax.Precision.HI...  12.4 us
    dot_general x1, matrix products, body(): jnp.einsum('nc,bnp->cbp', basis_table, pieces, precision=lax.Precision.HI...  10.9 us
  transfers between devices with their start and end apart: 3, of which 3 were waited for; matrix products, arithmetic and copies ran while one was open for 0% of the time, Pallas kernels for 0%

commit v1 on v0

--- a/solution.py
+++ b/solution.py
@@ -1,10 +1,17 @@
+import functools
+
 import jax
 import jax.numpy as jnp
+import numpy as np
 from jax import lax
+from jax.experimental import pallas as pl
+from jax.experimental.pallas import tpu as pltpu
 from jax.sharding import PartitionSpec as P
 
 NFFT = 256
 NBINS = 64
+LANES = 128
+MESH = pl.DeviceIdType.MESH
 
 
 def passed_along(array, axis, by):
@@ -71,9 +78,423 @@
     return spectra.transpose(1, 2, 0, 3)
 
 
+def tile_start(device, tiles, width_tm, space):
+    return (device * tiles + (space % 2) * (width_tm // 2)) // width_tm
+
+
+def halves(value):
+    high = value.astype(jnp.bfloat16)
+    return high, (value - high.astype(jnp.float32)).astype(jnp.bfloat16)
+
+
+def matmul(a, b):
+    return lax.dot_general(a, b, (((1,), (0,)), ((), ())), preferred_element_type=jnp.float32)
+
+
+def matmul_nt(a, b):
+    return lax.dot_general(a, b, (((1,), (1,)), ((), ())), preferred_element_type=jnp.float32)
+
+
+def exact(a, b):
+    return jnp.dot(a, b, precision=lax.Precision.HIGHEST, preferred_element_type=jnp.float32)
+
+
+def picked(selector, values):
+    high, low = halves(values)
+    return matmul(selector, high) + matmul(selector, low)
+
+
+def picked_right(values, selector):
+    high, low = halves(values)
+    return matmul(high, selector) + matmul(low, selector)
+
+
+def table_rows(bins, length):
+    shape = (bins.shape[0], length)
+    sample = lax.broadcasted_iota(jnp.int32, shape, 1)
+    odd = (lax.broadcasted_iota(jnp.int32, shape, 0) & 1) == 1
+    window = 0.5 - 0.5 * jnp.cos(2.0 * jnp.pi * sample.astype(jnp.float32) / length)
+    turns = (sample * bins) & (length - 1)
+    angle = 2.0 * jnp.pi * turns.astype(jnp.float32) / length
+    return window * jnp.where(odd, -jnp.sin(angle), jnp.cos(angle))
+
+
+def kernel(
+    n,
+    n_space,
+    snap_ref,
+    closing_ref,
+    weights_ref,
+    bins_ref,
+    left_ref,
+    even_ref,
+    odd_ref,
+    ones_ref,
+    out_ref,
+    series,
+    table_ref,
+    a_high,
+    a_low,
+    b_high,
+    b_low,
+    gram,
+    part,
+    rows_in,
+    mine,
+    spread,
+    local_sem,
+    send_sem,
+    recv_sem,
+    part_send,
+    part_recv,
+    space_send,
+    space_recv,
+):
+    me = lax.axis_index("tm")
+    here = lax.axis_index("space")
+    rows, points = snap_ref.shape
+    tail_rows = closing_ref.shape[0]
+    tiles = points // LANES
+    slots = series.shape[0]
+    hop = NFFT // 2
+    blocks_all = n * rows // hop
+    channels = bins_ref.shape[0]
+    group = channels // n
+
+    near = me // (n // 2) * (n // 2)
+    far = n // 2 - near
+
+    def peer_of(k):
+        return lax.rem(me + k, n)
+
+    def near_peer(k):
+        return near + lax.rem(me - near + k, n // 2)
+
+    def far_peer(k):
+        return far + lax.rem(me - near + k, n // 2)
+
+    peers_near = [near_peer(k) for k in range(1, n // 2)]
+    peers_far = [far_peer(k) for k in range(n // 2)]
+
+    def begin(device):
+        return tile_start(device, tiles, n, here)
+
+    def count(device):
+        return begin(device + 1) - begin(device)
+
+    my_start, my_count = begin(me), count(me)
+
+    def columns(tile):
+        return pl.ds(pl.multiple_of(tile * LANES, LANES), LANES)
+
+    def own_copies(t):
+        return (
+            pltpu.make_async_copy(
+                snap_ref.at[:, columns(my_start + t)],
+                series.at[t, pl.ds(pl.multiple_of(me * rows, rows), rows)],
+                local_sem.at[0, t],
+            ),
+            pltpu.make_async_copy(
+                closing_ref.at[:, columns(my_start + t)],
+                series.at[t, pl.ds(n * rows, tail_rows)],
+                local_sem.at[1, t],
+            ),
+        )
+
+    def outgoing(t, peer):
+        return pltpu.make_async_remote_copy(
+            src_ref=snap_ref.at[:, columns(begin(peer) + t)],
+            dst_ref=series.at[t, pl.ds(pl.multiple_of(me * rows, rows), rows)],
+            send_sem=send_sem.at[t, peer],
+            recv_sem=recv_sem.at[t, me],
+            device_id={"tm": peer},
+            device_id_type=MESH,
+        )
+
+    def incoming(t, peer):
+        return pltpu.make_async_remote_copy(
+            src_ref=snap_ref.at[:, columns(my_start + t)],
+            dst_ref=series.at[t, pl.ds(pl.multiple_of(peer * rows, rows), rows)],
+            send_sem=send_sem.at[t, peer],
+            recv_sem=recv_sem.at[t, peer],
+            device_id={"tm": peer},
+            device_id_type=MESH,
+        )
+
+    barrier = pltpu.get_barrier_semaphore()
+    for k in range(1, n):
+        pl.semaphore_signal(barrier, inc=1, device_id={"tm": peer_of(k)}, device_id_type=MESH)
+    for k in range(1, n_space):
+        pl.semaphore_signal(
+            barrier, inc=1, device_id={"space": lax.rem(here + k, n_space)}, device_id_type=MESH
+        )
+    pl.semaphore_wait(barrier, n - 1 + n_space - 1)
+
+    @pl.loop(0, slots)
+    def _(t):
+        for peer in [peer_of(k) for k in range(1, n)]:
+
+            @pl.when(t < count(peer))
+            def _(peer=peer):
+                outgoing(t, peer).start()
+
+        @pl.when(t < my_count)
+        def _():
+            for copy in own_copies(t):
+                copy.start()
+
+    @pl.when(my_count < slots)
+    def _():
+        series[slots - 1] = jnp.zeros(series.shape[1:], jnp.float32)
+
+    gram[...] = jnp.zeros(gram.shape, jnp.float32)
+    table_high, table_low = halves(table_rows(bins_ref[...], NFFT))
+    table_ref[:channels] = table_high
+    table_ref[channels:] = table_low
+
+    @pl.loop(0, slots // 2)
+    def _(step):
+        def arrived(peers, own):
+            for half in range(2):
+                t = 2 * step + half
+
+                @pl.when(t < my_count)
+                def _(t=t):
+                    if own:
+                        for copy in own_copies(t):
+                            copy.wait()
+                    for peer in peers:
+                        incoming(t, peer).wait_recv()
+
+        weight = []
+        for half in range(2):
+            t = 2 * step + half
+            held = weights_ref[pl.ds(jnp.minimum(my_start + t, tiles - 1), 1), :]
+            weight.append(held * (t < my_count).astype(jnp.float32))
+        weight = jnp.concatenate(weight, axis=1)
+
+        def transform(turn, carry):
+            block = lax.rem(near * (rows // hop) + turn, blocks_all)
+            window = pl.ds(pl.multiple_of(block * hop, hop), NFFT)
+            piece = jnp.concatenate(
+                [series[2 * step, window, :], series[2 * step + 1, window, :]], axis=1
+            )
+            high, low = halves(piece)
+            both = matmul(table_ref[...], high)
+            coef = both[:channels] + both[channels:] + matmul(table_ref[:channels], low)
+            first_high, first_low = halves(coef)
+            second_high, second_low = halves(coef * weight)
+            place = pl.ds(pl.multiple_of(block * group, group), group)
+            for g in range(n):
+                cut = slice(g * group, (g + 1) * group)
+                a_high[g, place, :] = first_high[cut]
+                a_low[g, place, :] = first_low[cut]
+                b_high[g, place, :] = second_high[cut]
+                b_low[g, place, :] = second_low[cut]
+            return carry
+
+        ready = blocks_all // 2 - 1
+        arrived(peers_near, True)
+        lax.fori_loop(0, ready, transform, 0, unroll=ready)
+        arrived(peers_far, False)
+        lax.fori_loop(ready, blocks_all, transform, 0, unroll=3)
+
+        def products(g, carry):
+            gram[g] += (
+                matmul_nt(b_high[g], a_high[g])
+                + matmul_nt(b_high[g], a_low[g])
+                + matmul_nt(b_low[g], a_high[g])
+            )
+            return carry
+
+        lax.fori_loop(0, n, products, 0, unroll=2)
+
+    size = gram.shape[1]
+    row = lax.broadcasted_iota(jnp.int32, (size, size), 0)
+    col = lax.broadcasted_iota(jnp.int32, (size, size), 1)
+    same_bin = ((row & (group - 1)) >> 1) == ((col & (group - 1)) >> 1)
+
+    def folded(g):
+        kept = picked(left_ref[...], jnp.where(same_bin, gram[g], 0.0))
+        middle = kept.shape[0] // 2
+        return picked_right(kept[:middle], even_ref[...]) + picked_right(
+            kept[middle:], odd_ref[...]
+        )
+
+    def part_copy(k):
+        peer = peer_of(k)
+        return pltpu.make_async_remote_copy(
+            src_ref=part.at[peer],
+            dst_ref=rows_in.at[me],
+            send_sem=part_send.at[peer],
+            recv_sem=part_recv.at[me],
+            device_id={"tm": peer},
+            device_id_type=MESH,
+        )
+
+    def part_arrival(k):
+        peer = peer_of(k)
+        return pltpu.make_async_remote_copy(
+            src_ref=part.at[peer],
+            dst_ref=rows_in.at[peer],
+            send_sem=part_send.at[peer],
+            recv_sem=part_recv.at[peer],
+            device_id={"tm": peer},
+            device_id_type=MESH,
+        )
+
+    for k in range(1, n):
+        part[peer_of(k)] = folded(peer_of(k))
+        part_copy(k).start()
+    rows_in[me] = folded(me)
+    for k in range(1, n):
+        part_arrival(k).wait_recv()
+    total = rows_in[0]
+    for p in range(1, n):
+        total = total + rows_in[p]
+    mine[...] = total
+    spread[here] = total
+
+    def space_copy(k):
+        peer = lax.rem(here + k, n_space)
+        return pltpu.make_async_remote_copy(
+            src_ref=mine,
+            dst_ref=spread.at[here],
+            send_sem=space_send.at[peer],
+            recv_sem=space_recv.at[here],
+            device_id={"space": peer},
+            device_id_type=MESH,
+        )
+
+    def space_arrival(k):
+        peer = lax.rem(here + k, n_space)
+        return pltpu.make_async_remote_copy(
+            src_ref=mine,
+            dst_ref=spread.at[peer],
+            send_sem=space_send.at[peer],
+            recv_sem=space_recv.at[peer],
+            device_id={"space": peer},
+            device_id_type=MESH,
+        )
+
+    for k in range(1, n_space):
+        space_copy(k).start()
+    for k in range(1, n_space):
+        space_arrival(k).wait_recv()
+    total = spread[0]
+    for p in range(1, n_space):
+        total = total + spread[p]
+    line = lax.broadcasted_iota(jnp.int32, total.shape, 0)
+    lane = lax.broadcasted_iota(jnp.int32, total.shape, 1)
+    diagonal = jnp.where(line == (lane & (blocks_all - 1)), total, 0.0)
+    trace = jnp.sum(diagonal, axis=0, keepdims=True)
+    energy = exact(jnp.broadcast_to(trace, (8, trace.shape[1])), ones_ref[...])[:1]
+    out_ref[...] = total * (blocks_all / energy)
+
+    @pl.loop(0, slots)
+    def _(t):
+        for k in range(1, n):
+            peer = peer_of(k)
+
+            @pl.when(t < count(peer))
+            def _():
+                outgoing(t, peer).wait_send()
+
+    for k in range(1, n):
+        part_copy(k).wait_send()
+    for k in range(1, n_space):
+        space_copy(k).wait_send()
+
+
+def selections(blocks, group):
+    size, bins = blocks * group, group // 2
+    block, channel = np.divmod(np.arange(size), group)
+    part, second = np.divmod(np.arange(2 * blocks), blocks)
+    match = second[:, None] == block[None, :]
+    first_half = match & (channel[None, :] % 2 == part[:, None])
+    second_half = match & (channel[None, :] % 2 == 1 - part[:, None])
+    sign = np.where(part[:, None] == 0, 1.0, -1.0)
+    left = np.concatenate([first_half * 1.0, second_half * sign], axis=0)
+    bin_of, first = np.divmod(np.arange(bins * blocks), blocks)
+    place = (block[:, None] == first[None, :]) & (channel[:, None] // 2 == bin_of[None, :])
+    even = place & (channel[:, None] % 2 == 0)
+    odd = place & (channel[:, None] % 2 == 1)
+    ones = bin_of[:, None] == bin_of[None, :]
+    return [jnp.asarray(m, jnp.bfloat16) for m in (left, even, odd)] + [
+        jnp.asarray(ones, jnp.float32)
+    ]
+
+
+def fused_body(snapshots, closing, weights, bin_index):
+    n, n_space = lax.axis_size("tm"), lax.axis_size("space")
+    rows, points = snapshots.shape
+    tail_rows = closing.shape[0]
+    tiles = points // LANES
+    slots = -(-tiles // n)
+    blocks_all = n * rows // (NFFT // 2)
+    channels = 2 * NBINS
+    group = channels // n
+    size = blocks_all * group
+    shape = (2 * blocks_all, size // 2)
+    whole = pl.BlockSpec(memory_space=pltpu.VMEM)
+    spread = pl.pallas_call(
+        functools.partial(kernel, n, n_space),
+        out_shape=jax.ShapeDtypeStruct(shape, jnp.float32),
+        in_specs=[pl.BlockSpec(memory_space=pl.ANY)] * 2 + [whole] * 6,
+        out_specs=whole,
+        scratch_shapes=[
+            pltpu.VMEM((slots, n * rows + tail_rows, LANES), jnp.float32),
+            pltpu.VMEM((2 * channels, NFFT), jnp.bfloat16),
+        ]
+        + [pltpu.VMEM((n, size, 2 * LANES), jnp.bfloat16)] * 4
+        + [
+            pltpu.VMEM((n, size, size), jnp.float32),
+            pltpu.VMEM((n,) + shape, jnp.float32),
+            pltpu.VMEM((n,) + shape, jnp.float32),
+            pltpu.VMEM(shape, jnp.float32),
+            pltpu.VMEM((n_space,) + shape, jnp.float32),
+            pltpu.SemaphoreType.DMA((2, slots)),
+            pltpu.SemaphoreType.DMA((slots, n)),
+            pltpu.SemaphoreType.DMA((slots, n)),
+            pltpu.SemaphoreType.DMA((n,)),
+            pltpu.SemaphoreType.DMA((n,)),
+            pltpu.SemaphoreType.DMA((n_space,)),
+            pltpu.SemaphoreType.DMA((n_space,)),
+        ],
+        compiler_params=pltpu.CompilerParams(collective_id=0, has_side_effects=True),
+    )(
+        snapshots,
+        closing,
+        weights.reshape(tiles, LANES),
+        jnp.repeat(bin_index, 2)[:, None],
+        *selections(blocks_all, group),
+    )
+    by_pair = spread.reshape(2, blocks_all, group // 2, blocks_all).transpose(2, 0, 3, 1)
+    own_rows = blocks_all // n_space
+    return lax.dynamic_slice_in_dim(by_pair, lax.axis_index("space") * own_rows, own_rows, 2)
+
+
+def chosen_body(snapshots, closing, weights, bin_index):
+    n = lax.axis_size("tm")
+    rows, points = snapshots.shape
+    group = 2 * NBINS // n
+    blocks_all = n * rows // (NFFT // 2)
+    slots = -(-(points // LANES) // n)
+    fits = (
+        2 * NBINS % n == 0
+        and n % 2 == 0
+        and points % LANES == 0
+        and slots % 2 == 0
+        and closing.shape[0] == NFFT // 2
+        and group == 16
+        and blocks_all == 16
+    )
+    return (fused_body if fits else body)(snapshots, closing, weights, bin_index)
+
+
 def solution(mesh):
     return jax.shard_map(
-        body,
+        chosen_body,
         mesh=mesh,
         in_specs=(P("tm", "space"), P(None, "space"), P("space"), P()),
         out_specs=P("tm", None, "space", None),

time: 408 us -> 195 us (0.48)
  waiting for transfers between devices: 278 us -> 0 us
  Pallas kernels: 0 us -> 191 us
  matrix products: 47 us -> 0 us
  local copies, waits for them, and re-layouts: 45.6 us -> 3.12 us
  between operations: 13.5 us -> 0.03 us
  other arithmetic: 9.88 us -> 0 us
  starting transfers between devices: 7.25 us -> 0 us
  blocking collectives: 5.74 us -> 0 us
    pallas_call x0 -> x1, Pallas kernels: none -> 191 us  [fused_body(): pl.pallas_call(functools.partial(kernel, n, n_space), out_shape=jax.Shape...]
    all_to_all x1 -> x0, waiting for transfers between devices: 171 us -> none  [body(): lax.all_to_all(spectrum, 'tm', split_axis=0, concat_axis=2, tiled=True)]
    ppermute x1 -> x0, waiting for transfers between devices: 88.1 us -> none  [passed_along(): return lax.ppermute(array, axis, pairs)]
    dot_general x3 -> x0, matrix products: 47 us -> none  [the longest x1 35.3 us: cross_spectra(): jnp.einsum('kaip,kbjp->kabij', first_set, second_set, precision=lax.Preci...]
    all_to_all x3 -> x0, local copies, waits for them, and re-layouts: 27 us -> none  [body(): lax.all_to_all(spectrum, 'tm', split_axis=0, concat_axis=2, tiled=True)]
    reduce_scatter x1 -> x0, waiting for transfers between devices: 18.8 us -> none  [body(): lax.psum_scatter(cross_spectra(gathered, weighted).transpose(2, 0, 1, 3),...]
    dot_general x2 -> x0, local copies, waits for them, and re-layouts: 12.4 us -> none  [body(): jnp.einsum('nc,bnp->cbp', basis_table, pieces, precision=lax.Precision.HI...]
    all_to_all x1 -> x0, starting transfers between devices: 5.93 us -> none  [body(): lax.all_to_all(spectrum, 'tm', split_axis=0, concat_axis=2, tiled=True)]
  transfers between devices with their start and end apart: 3 -> 0, of which waited for: 3 -> 0; matrix products, arithmetic and copies ran while one was open for 0% -> 0% of each run, Pallas kernels for 0% -> 0%
where the time goes in v1:
time: 195 us
  Pallas kernels  191 us (98%)
  local copies, waits for them, and re-layouts  3.12 us (2%)
    pallas_call x1, Pallas kernels, fused_body(): pl.pallas_call(functools.partial(kernel, n, n_space), out_shape=jax.Shape...  191 us

profile of v1, /device:TPU:0, one launch (start us, length us, event | category | flops | bytes accessed | tf_op | source)
XLA Modules:
  0.0 194.6 jit_solution(2872004686122116516)
XLA Ops:
  0.0 0.7 broadcast_in_dim.3
  0.7 0.7 broadcast_in_dim_reshape.4.bins_ref
  1.4 191.4 %shard_map.82 = f32[32,128]{1,0:T(8,128)} custom-call(f32[256,7680]{1,0:T(8,128)} %snap_ref.1, f32[128,7680]{1,0:T(8,128)} %closing_ref.1, f32[60,128]{1,0:T(8,128)} %bitcast.2, s32[128,1]{1,0:T(8,128)} %broadcast_in_dim_reshape.4.bins_ref, bf16[64,256]{1,0:T(8,128)(2,1)} %constant.19.clone.left_ref, bf16[256,128]{1,0:T(8,128)(2,1)} %constant.20.clone.even_ref, ...), custom_call_target="tpu_custom_call" | custom-call | tf_op jit(solution)/shard_map/pallas_call | solution.py:440
  192.9 0.8 reshape.7
  193.7 0.1 constant_dynamic-slice_fusion
  193.8 0.8 copy.13
